TPU v7x, 32 devices: a whole 2x2x4 slice. The times are simulated.
32 devices in a mesh: shot: 4 (over y, x), rcv: 8 (over z, core).
Axes of the slice: x: 2, y: 2, z: 4, core: 2. Of those that a mesh axis runs over, the one named last changes fastest.
Arguments:
- modeled: bfloat16 [2, 32, 4, 64, 512], P(None, 'shot', None, 'rcv'), may hold values from -9 to 9
- observed: bfloat16 [2, 4, 32, 64, 512], P(None, 'shot', 'rcv'), may hold values from -60 to 60
- mask: int32 [32, 4, 64], P('shot', None, 'rcv'), may hold values 0 or 1
- shot_order: int32 [32], replicated, may hold values from 0 to 31, as said below
- line_of_slot: int32 [4], replicated, may hold values from 0 to 3, as said below
- coupling: bfloat16 [2, 512, 512], replicated, may hold values from -0.25 to 0.25
- wavelet: float32 [2, 512], replicated, may hold values from -4 to 4
- damping: float32 [512], replicated, may hold values from 2048 to 32768
Outputs:
- new_wavelet: float32 [2, 512], replicated
- residual_out: bfloat16 [2, 32, 4, 64, 512], P(None, 'shot', None, 'rcv')
Inputs may be any that keep to these rules, and one draw needn't show every extreme that they name: Group g holds the shots shot_order[g * 8] to shot_order[(g + 1) * 8 - 1]; each shot number appears once. `line_of_slot`: each line appears in exactly one slot.
All inputs are finite; a program needn't handle non-finite values. No bound on the sum of `mask` on one device may be relied on, other than what follows from the above.
Results may differ from a plain program's by a relative error of at most 0.00045.
Values may be sent and summed in bfloat16 or wider, within the bound.
A program may use at most 64 MiB of HBM per device.

v0:
```python
import jax
import jax.numpy as jnp
from jax import lax
from jax.sharding import PartitionSpec as P


def weigh(trace, coupling):
    real_part = jnp.dot(trace[0], coupling[0], preferred_element_type=jnp.float32) - jnp.dot(
        trace[1], coupling[1], preferred_element_type=jnp.float32
    )
    imag_part = jnp.dot(trace[0], coupling[1], preferred_element_type=jnp.float32) + jnp.dot(
        trace[1], coupling[0], preferred_element_type=jnp.float32
    )
    return jnp.stack([real_part, imag_part])


def per_device(modeled, observed, mask, shot_order, line_of_slot, coupling, wavelet, damping):
    group_size = modeled.shape[1]
    line_count = modeled.shape[2]
    slot_count = lax.axis_size("shot")
    stored = observed[:, 0]
    spread = lax.all_to_all(stored, "rcv", split_axis=2, concat_axis=1, tiled=True)
    grouped = jnp.take(spread, shot_order, axis=1)
    grouped = grouped.reshape(2, slot_count, group_size, grouped.shape[2], grouped.shape[3])
    arrived = lax.all_to_all(grouped, "shot", split_axis=1, concat_axis=1, tiled=True)
    inverse = (
        jnp.zeros((line_count,), jnp.int32)
        .at[line_of_slot]
        .set(jnp.arange(line_count, dtype=jnp.int32))
    )
    by_line = jnp.transpose(jnp.take(arrived, inverse, axis=1), (0, 2, 1, 3, 4))
    wd = weigh(by_line, coupling)
    wg = weigh(modeled, coupling)
    live = mask.astype(jnp.float32)[..., None]
    res_re = live * (wd[0] - (wavelet[0] * wg[0] - wavelet[1] * wg[1]))
    res_im = live * (wd[1] - (wavelet[0] * wg[1] + wavelet[1] * wg[0]))
    num_re = jnp.sum(wg[0] * res_re + wg[1] * res_im, axis=(0, 1, 2))
    num_im = jnp.sum(wg[0] * res_im - wg[1] * res_re, axis=(0, 1, 2))
    den = jnp.sum(live * (wg[0] * wg[0] + wg[1] * wg[1]), axis=(0, 1, 2))
    numerator = jnp.stack([num_re, num_im])
    numerator, den = lax.psum((numerator, den), ("shot", "rcv"))
    new_wavelet = wavelet + numerator / (den + damping)[None, :]
    out_re = live * (wd[0] - (new_wavelet[0] * wg[0] - new_wavelet[1] * wg[1]))
    out_im = live * (wd[1] - (new_wavelet[0] * wg[1] + new_wavelet[1] * wg[0]))
    return (new_wavelet, jnp.stack([out_re, out_im]).astype(jnp.bfloat16))


def solution(mesh):
    placed = (
        P(None, "shot", None, "rcv", None),
        P(None, "shot", "rcv", None, None),
        P("shot", None, "rcv"),
        P(),
        P(),
        P(),
        P(),
        P(),
    )
    return jax.shard_map(
        per_device,
        mesh=mesh,
        in_specs=placed,
        out_specs=(P(), P(None, "shot", None, "rcv", None)),
        check_vma=False,
    )
```

profile of v0, /device:TPU:10, one launch (start us, length us, event | category | flops | bytes accessed | tf_op | source)
XLA Modules:
  0.0 82.5 jit_solution(1885239426793906169)
XLA Ops:
  0.6 0.0 copy-start
  0.6 2.3 %copy.30 = bf16[2,1,4,64,512]{4,2,0,3,1:T(4,128)(2,1)} copy(bf16[2,1,4,64,512]{4,3,2,1,0:T(8,128)(2,1)} %param.9) | data formatting | bytes 1048576 | tf_op args[1]
  3.0 0.0 copy-start.7
  3.0 0.0 copy-start.1
  3.0 5.5 %all-to-all-start = ((bf16[2,4,64,512]{3,1,0,2:T(4,128)(2,1)}), bf16[2,4,64,512]{3,1,0,2:T(4,128)(2,1)S(1)}, u32[]{:S(2)}, u32[]{:S(2)}) async-start(bf16[2,4,64,512]{3,1,0,2:T(4,128)(2,1)} %bitcast.71), calls=%async_computation | async-start | bytes 1048576 | tf_op jit(solution)/shard_map/all_to_all | solution.py:22
  8.4 0.0 copy-done.7
  8.4 0.0 copy-start.8
  8.5 0.6 copy-done.8
  9.1 0.1 broadcast_in_dim.31
  9.2 0.0 copy-start.3
  9.2 0.6 scatter_custom_fusion
  9.8 0.1 copy-done.3
  9.9 0.0 copy-done
  9.9 0.0 copy-done.1
  9.9 1.1 %fusion.2 = f32[8,4,8,512]{3,2,1,0:T(8,128)} fusion(bf16[2,512,512]{2,1,0:T(8,128)(2,1)S(1)} %copy-done, bf16[2,8,4,8,512]{4,3,2,1,0:T(8,128)(2,1)S(1)} %copy-done.1), kind=kOutput, calls=%fused_computation.10 | convolution fusion | flops 134217728 | bytes 1310720 | tf_op jit(solution)/shard_map/dot_general | solution.py:11
  11.0 0.3 fusion.10
  11.3 9.2 %all-to-all-done = bf16[2,4,64,512]{3,1,0,2:T(4,128)(2,1)S(1)} async-done(((bf16[2,4,64,512]{3,1,0,2:T(4,128)(2,1)}), bf16[2,4,64,512]{3,1,0,2:T(4,128)(2,1)S(1)}, u32[]{:S(2)}, u32[]{:S(2)}) %all-to-all-start) | async-done | bytes 524320 | tf_op jit(solution)/shard_map/all_to_all | solution.py:22
  20.5 0.2 copy.29
  20.7 0.6 gather_fusion
  21.3 0.9 %copy_select_fusion.1 = bf16[2,4,8,8,512]{4,3,2,0,1:T(8,128)(2,1)} fusion(bf16[2,4,8,8,512]{4,3,0,2,1:T(8,128)(2,1)S(1)} %bitcast.75, pred[4,8]{1,0:T(4,128)(4,1)S(1)} %broadcast_in_dim.31), kind=kLoop, calls=%fused_computation.22 | loop fusion | flops 262144 | bytes 1048608 | tf_op jit(solution)/shard_map/jit(_take)/select_n | solution.py:23
  22.2 0.0 copy-start.5
  22.3 4.4 %all-to-all-start.1 = ((bf16[2,4,8,8,512]{4,3,2,0,1:T(8,128)(2,1)}), bf16[2,4,8,8,512]{4,3,2,0,1:T(8,128)(2,1)S(1)}, u32[]{:S(2)}, u32[]{:S(2)}) async-start(bf16[2,4,8,8,512]{4,3,2,0,1:T(8,128)(2,1)} %copy_select_fusion.1), calls=%async_computation.1 | async-start | bytes 1048576 | tf_op jit(solution)/shard_map/all_to_all | solution.py:25
  26.6 0.0 copy-done.5
  26.7 0.3 convolution_subtract_fusion.1
  27.0 7.1 %all-to-all-done.1 = bf16[2,4,8,8,512]{4,3,2,0,1:T(8,128)(2,1)S(1)} async-done(((bf16[2,4,8,8,512]{4,3,2,0,1:T(8,128)(2,1)}), bf16[2,4,8,8,512]{4,3,2,0,1:T(8,128)(2,1)S(1)}, u32[]{:S(2)}, u32[]{:S(2)}) %all-to-all-start.1) | async-done | bytes 524320 | tf_op jit(solution)/shard_map/all_to_all | solution.py:25
  34.1 0.6 gather_fusion.1
  34.7 0.1 fusion.12
  34.8 0.3 fusion
  35.1 0.3 fusion.8
  35.4 0.3 convolution_add_fusion
  35.7 0.0 copy-start.2
  35.7 0.3 convolution_subtract_fusion
  36.0 0.7 copy-done.2
  36.8 0.0 copy-start.6
  36.8 1.4 %add_reduce_fusion = (f32[512]{0:T(512)S(1)}, f32[512]{0:T(512)S(1)}, f32[512]{0:T(512)S(1)}, f32[8,4,8,512]{3,2,1,0:T(8,128)}) fusion(f32[8,4,8,512]{3,2,1,0:T(8,128)S(1)} %convolution_add_fusion, f32[8,4,8,512]{3,2,1,0:T(8,128)S(1)} %convolution_subtract_fusion.1, f32[8,4,8,512]{3,2,1,0:T(8,128)S(1)} %convolution_subtract_fusion, f32[512]{0:T(512)S(1)} %bitcast.79, ...), kind=kOutput, calls=%fused_computation.29 | convolution fusion | flops 137361920 | bytes 3434496 | tf_op jit(solution)/shard_map/dot_general | solution.py:11
  38.2 41.5 %all-reduce = (f32[2,512]{1,0:T(2,128)S(1)}, f32[512]{0:T(512)S(1)}) all-reduce(f32[2,512]{1,0:T(2,128)S(1)} %pad_maximum_fusion.1, f32[512]{0:T(512)S(1)} %get-tuple-element.4), channel_id=1, replica_groups=mesh['shot'=4,'rcv'=8] {'shot','rcv'}, use_global_device_ids=true, to_apply=%region_3.4 | all-reduce | flops 1536 | bytes 12288 | tf_op jit(solution)/shard_map/psum | solution.py:41
  79.7 0.0 copy-done.6
  79.8 0.0 copy-start.4
  79.8 0.6 copy-done.4
  80.4 1.3 %fusion.21 = (bf16[1,8,4,8,512]{4,3,2,1,0:T(8,128)(2,1)S(1)}, bf16[1,8,4,8,512]{4,3,2,1,0:T(8,128)(2,1)S(1)}) fusion(f32[8,4,8,512]{3,2,1,0:T(8,128)S(1)} %convolution_subtract_fusion, f32[8,4,8,512]{3,2,1,0:T(8,128)} %get-tuple-element.13, f32[8,4,8,512]{3,2,1,0:T(8,128)S(1)} %convolution_subtract_fusion.1, f32[512]{0:T(512)S(1)} %bitcast.77, ...), kind=kLoop, calls=%fused_computation.40 | loop fusion | flops 1572864 | bytes 2626560 | tf_op jit(solution)/shard_map/stack | solution.py:45
  81.6 0.8 %pad_maximum_fusion = bf16[2,8,4,8,512]{4,3,2,1,0:T(8,128)(2,1)} fusion(bf16[1,8,4,8,512]{4,3,2,1,0:T(8,128)(2,1)S(1)} %get-tuple-element.8, bf16[1,8,4,8,512]{4,3,2,1,0:T(8,128)(2,1)S(1)} %get-tuple-element.7), kind=kLoop, calls=%fused_computation.7 | loop fusion | flops 262144 | bytes 1048576 | tf_op jit(solution)/shard_map/stack | solution.py:45
  (16 shorter events, 0.2 us)
Async XLA Ops:
  0.6 9.3 %copy-start = (bf16[2,512,512]{2,1,0:T(8,128)(2,1)S(1)}, bf16[2,512,512]{2,1,0:T(8,128)(2,1)}, u32[]{:S(2)}) copy-start(bf16[2,512,512]{2,1,0:T(8,128)(2,1)} %param.13) | copy-start | bytes 3145732
  3.0 5.5 %copy-start.7 = (s32[32]{0:T(128)S(1)}, s32[32]{0:T(128)}, u32[]{:S(2)}) copy-start(s32[32]{0:T(128)} %param.11) | copy-start | bytes 388
  3.0 6.9 %copy-start.1 = (bf16[2,8,4,8,512]{4,3,2,1,0:T(8,128)(2,1)S(1)}, bf16[2,8,4,8,512]{4,3,2,1,0:T(8,128)(2,1)}, u32[]{:S(2)}) copy-start(bf16[2,8,4,8,512]{4,3,2,1,0:T(8,128)(2,1)} %param.8) | copy-start | bytes 1572868
  3.0 17.6 %all-to-all-start = ((bf16[2,4,64,512]{3,1,0,2:T(4,128)(2,1)}), bf16[2,4,64,512]{3,1,0,2:T(4,128)(2,1)S(1)}, u32[]{:S(2)}, u32[]{:S(2)}) async-start(bf16[2,4,64,512]{3,1,0,2:T(4,128)(2,1)} %bitcast.71), calls=%async_computation | async-start | bytes 1048576 | tf_op jit(solution)/shard_map/all_to_all | solution.py:22
  8.4 0.7 copy-start.8
  9.2 0.7 copy-start.3
  22.2 4.4 %copy-start.5 = (s32[8,4,8]{2,1,0:T(4,128)S(1)}, s32[8,4,8]{2,1,0:T(4,128)}, u32[]{:S(2)}) copy-start(s32[8,4,8]{2,1,0:T(4,128)} %param.10) | copy-start | bytes 3076
  22.3 11.8 %all-to-all-start.1 = ((bf16[2,4,8,8,512]{4,3,2,0,1:T(8,128)(2,1)}), bf16[2,4,8,8,512]{4,3,2,0,1:T(8,128)(2,1)S(1)}, u32[]{:S(2)}, u32[]{:S(2)}) async-start(bf16[2,4,8,8,512]{4,3,2,0,1:T(8,128)(2,1)} %copy_select_fusion.1), calls=%async_computation.1 | async-start | bytes 1048576 | tf_op jit(solution)/shard_map/all_to_all | solution.py:25
  35.7 1.0 %copy-start.2 = (f32[8,4,8,512]{3,2,1,0:T(8,128)S(1)}, f32[8,4,8,512]{3,2,1,0:T(8,128)}, u32[]{:S(2)}) copy-start(f32[8,4,8,512]{3,2,1,0:T(8,128)} %fusion.2) | copy-start | bytes 1572868
  36.8 43.0 %copy-start.6 = (f32[512]{0:T(512)S(1)}, f32[512]{0:T(512)}, u32[]{:S(2)}) copy-start(f32[512]{0:T(512)} %param.15) | copy-start | bytes 6148
  79.8 0.6 copy-start.4
where the time goes:
time: 83 us; the launch traced here: 82.5 us
  blocking collectives  41.5 us (50%)
  waiting for transfers between devices  16.3 us (20%)
  starting transfers between devices  9.83 us (12%)
  local copies, waits for them, and re-layouts  6.43 us (8%)
  matrix products  4.33 us (5%)
  other arithmetic  3.19 us (4%)
    psum x1, blocking collectives, per_device(): numerator, den = lax.psum((numerator, den), ('shot', 'rcv'))  41.5 us
    all_to_all x1, waiting for transfers between devices, per_device(): lax.all_to_all(stored, 'rcv', split_axis=2, concat_axis=1, tiled=True)  9.24 us
    all_to_all x1, waiting for transfers between devices, per_device(): lax.all_to_all(grouped, 'shot', split_axis=1, concat_axis=1, tiled=True)  7.09 us
    all_to_all x1, starting transfers between devices, per_device(): lax.all_to_all(stored, 'rcv', split_axis=2, concat_axis=1, tiled=True)  5.45 us
    all_to_all x1, starting transfers between devices, per_device(): lax.all_to_all(grouped, 'shot', split_axis=1, concat_axis=1, tiled=True)  4.38 us
    unnamed x19, local copies, waits for them, and re-layouts  4.35 us
    another operation x2, other arithmetic, per_device(): return (new_wavelet, jnp.stack([out_re, out_im]).astype(jnp.bfloat16))  2.1 us
    dot_general x2, matrix products, weigh(): jnp.dot(trace[1], coupling[0], preferred_element_type=jnp.float32)  1.73 us
  transfers between devices with their start and end apart: 2, of which 2 were waited for; matrix products, arithmetic and copies ran while one was open for 3% of the time, Pallas kernels for 0%

commit v1 on v0

--- a/solution.py
+++ b/solution.py
@@ -22,7 +22,9 @@
     spread = lax.all_to_all(stored, "rcv", split_axis=2, concat_axis=1, tiled=True)
     grouped = jnp.take(spread, shot_order, axis=1)
     grouped = grouped.reshape(2, slot_count, group_size, grouped.shape[2], grouped.shape[3])
-    arrived = lax.all_to_all(grouped, "shot", split_axis=1, concat_axis=1, tiled=True)
+    pieces = jnp.split(grouped, lax.axis_size("shot"), axis=1)
+    received = lax.all_to_all(jnp.stack(pieces), "shot", 0, 0)
+    arrived = jnp.concatenate(received, axis=1)
     inverse = (
         jnp.zeros((line_count,), jnp.int32)
         .at[line_of_slot]

time: 83 us -> 83.1 us (level)
    another operation x0 -> x1, other arithmetic: none -> 0.86 us  [per_device(): received = lax.all_to_all(jnp.stack(pieces), 'shot', 0, 0)]
where the time goes in v1:
time: 83.1 us; the launch traced here: 82.6 us
  blocking collectives  41.5 us (50%)
  waiting for transfers between devices  16.3 us (20%)
  starting transfers between devices  9.83 us (12%)
  local copies, waits for them, and re-layouts  6.46 us (8%)
  matrix products  4.32 us (5%)
  other arithmetic  3.26 us (4%)
    psum x1, blocking collectives, per_device(): numerator, den = lax.psum((numerator, den), ('shot', 'rcv'))  41.5 us
    all_to_all x1, waiting for transfers between devices, per_device(): lax.all_to_all(stored, 'rcv', split_axis=2, concat_axis=1, tiled=True)  9.26 us
    all_to_all x1, waiting for transfers between devices, per_device(): received = lax.all_to_all(jnp.stack(pieces), 'shot', 0, 0)  7.09 us
    all_to_all x1, starting transfers between devices, per_device(): lax.all_to_all(stored, 'rcv', split_axis=2, concat_axis=1, tiled=True)  5.45 us
    all_to_all x1, starting transfers between devices, per_device(): received = lax.all_to_all(jnp.stack(pieces), 'shot', 0, 0)  4.38 us
    unnamed x19, local copies, waits for them, and re-layouts  4.35 us
    another operation x2, other arithmetic, per_device(): return (new_wavelet, jnp.stack([out_re, out_im]).astype(jnp.bfloat16))  2.1 us
    dot_general x2, matrix products, weigh(): jnp.dot(trace[1], coupling[0], preferred_element_type=jnp.float32)  1.73 us
  transfers between devices with their start and end apart: 2, of which 2 were waited for; matrix products, arithmetic and copies ran while one was open for 3% of the time, Pallas kernels for 0%

profile of v1, /device:TPU:10, one launch (start us, length us, event | category | flops | bytes accessed | tf_op | source)
XLA Modules:
  0.0 82.6 jit_solution(17346934182558155640)
XLA Ops:
  0.6 0.0 copy-start
  0.6 2.3 %copy.41 = bf16[2,1,4,64,512]{4,2,0,3,1:T(4,128)(2,1)} copy(bf16[2,1,4,64,512]{4,3,2,1,0:T(8,128)(2,1)} %param.9) | data formatting | bytes 1048576 | tf_op args[1]
  3.0 0.0 copy-start.7
  3.0 0.0 copy-start.1
  3.0 5.5 %all-to-all-start = ((bf16[2,4,64,512]{3,1,0,2:T(4,128)(2,1)}), bf16[2,4,64,512]{3,1,0,2:T(4,128)(2,1)S(1)}, u32[]{:S(2)}, u32[]{:S(2)}) async-start(bf16[2,4,64,512]{3,1,0,2:T(4,128)(2,1)} %bitcast.84), calls=%async_computation | async-start | bytes 1048576 | tf_op jit(solution)/shard_map/all_to_all | solution.py:22
  8.4 0.0 copy-done.7
  8.4 0.0 copy-start.8
  8.5 0.6 copy-done.8
  9.1 0.1 broadcast_in_dim.31
  9.2 0.0 copy-start.3
  9.2 0.6 scatter_custom_fusion
  9.8 0.1 copy-done.3
  9.9 0.0 copy-done
  9.9 0.0 copy-done.1
  9.9 1.1 %fusion.2 = f32[8,4,8,512]{3,2,1,0:T(8,128)} fusion(bf16[2,512,512]{2,1,0:T(8,128)(2,1)S(1)} %copy-done, bf16[2,8,4,8,512]{4,3,2,1,0:T(8,128)(2,1)S(1)} %copy-done.1), kind=kOutput, calls=%fused_computation.11 | convolution fusion | flops 134217728 | bytes 1310720 | tf_op jit(solution)/shard_map/dot_general | solution.py:11
  11.0 0.3 fusion.10
  11.3 9.3 %all-to-all-done = bf16[2,4,64,512]{3,1,0,2:T(4,128)(2,1)S(1)} async-done(((bf16[2,4,64,512]{3,1,0,2:T(4,128)(2,1)}), bf16[2,4,64,512]{3,1,0,2:T(4,128)(2,1)S(1)}, u32[]{:S(2)}, u32[]{:S(2)}) %all-to-all-start) | async-done | bytes 524320 | tf_op jit(solution)/shard_map/all_to_all | solution.py:22
  20.5 0.2 copy.40
  20.7 0.6 gather_fusion
  21.3 0.1 copy_select_fusion.1
  21.5 0.9 %pad_maximum_fusion = bf16[4,2,1,8,8,512]{5,4,3,1,2,0:T(8,128)(2,1)} fusion(bf16[1,2,1,8,8,512]{5,4,3,1,2,0:T(8,128)(2,1)S(1)} %get-tuple-element.10, bf16[1,2,1,8,8,512]{5,4,3,1,2,0:T(8,128)(2,1)S(1)} %get-tuple-element.11, bf16[1,2,1,8,8,512]{5,4,3,1,2,0:T(8,128)(2,1)S(1)} %get-tuple-element.12, bf16[1,2,1,8,8,512]{5,4,3,1,2,0:T(8,128)(2,1)S(1)} %get-tuple-element.9), kind=kLoop, calls=%fused_computation.7 | loop fusion | flops 786432 | bytes 1048576 | tf_op jit(solution)/shard_map/stack | solution.py:26
  22.4 0.0 copy-start.5
  22.4 4.4 %all-to-all-start.1 = ((bf16[4,2,1,8,8,512]{5,4,3,1,2,0:T(8,128)(2,1)}), bf16[4,2,1,8,8,512]{5,4,3,1,2,0:T(8,128)(2,1)S(1)}, u32[]{:S(2)}, u32[]{:S(2)}) async-start(bf16[4,2,1,8,8,512]{5,4,3,1,2,0:T(8,128)(2,1)} %pad_maximum_fusion), calls=%async_computation.1 | async-start | bytes 1048576 | tf_op jit(solution)/shard_map/all_to_all | solution.py:26
  26.8 0.0 copy-done.5
  26.8 0.3 convolution_subtract_fusion.1
  27.1 7.1 %all-to-all-done.1 = bf16[4,2,1,8,8,512]{5,4,3,1,2,0:T(8,128)(2,1)S(1)} async-done(((bf16[4,2,1,8,8,512]{5,4,3,1,2,0:T(8,128)(2,1)}), bf16[4,2,1,8,8,512]{5,4,3,1,2,0:T(8,128)(2,1)S(1)}, u32[]{:S(2)}, u32[]{:S(2)}) %all-to-all-start.1) | async-done | bytes 524320 | tf_op jit(solution)/shard_map/all_to_all | solution.py:26
  34.2 0.6 gather_fusion.1
  34.8 0.1 fusion.12
  34.9 0.3 fusion
  35.2 0.3 fusion.8
  35.5 0.3 convolution_add_fusion
  35.8 0.0 copy-start.2
  35.9 0.3 convolution_subtract_fusion
  36.2 0.7 copy-done.2
  36.9 0.0 copy-start.6
  36.9 1.4 %add_reduce_fusion = (f32[512]{0:T(512)S(1)}, f32[512]{0:T(512)S(1)}, f32[512]{0:T(512)S(1)}, f32[8,4,8,512]{3,2,1,0:T(8,128)}) fusion(f32[8,4,8,512]{3,2,1,0:T(8,128)S(1)} %convolution_add_fusion, f32[8,4,8,512]{3,2,1,0:T(8,128)S(1)} %convolution_subtract_fusion.1, f32[8,4,8,512]{3,2,1,0:T(8,128)S(1)} %convolution_subtract_fusion, f32[512]{0:T(512)S(1)} %bitcast.93, ...), kind=kOutput, calls=%fused_computation.31 | convolution fusion | flops 137361920 | bytes 3434496 | tf_op jit(solution)/shard_map/dot_general | solution.py:11
  38.3 41.5 %all-reduce = (f32[2,512]{1,0:T(2,128)S(1)}, f32[512]{0:T(512)S(1)}) all-reduce(f32[2,512]{1,0:T(2,128)S(1)} %pad_maximum_fusion.2, f32[512]{0:T(512)S(1)} %get-tuple-element.4), channel_id=1, replica_groups=mesh['shot'=4,'rcv'=8] {'shot','rcv'}, use_global_device_ids=true, to_apply=%region_3.4 | all-reduce | flops 1536 | bytes 12288 | tf_op jit(solution)/shard_map/psum | solution.py:43
  79.9 0.0 copy-done.6
  79.9 0.0 copy-start.4
  79.9 0.6 copy-done.4
  80.5 1.3 %fusion.21 = (bf16[1,8,4,8,512]{4,3,2,1,0:T(8,128)(2,1)S(1)}, bf16[1,8,4,8,512]{4,3,2,1,0:T(8,128)(2,1)S(1)}) fusion(f32[8,4,8,512]{3,2,1,0:T(8,128)S(1)} %convolution_subtract_fusion, f32[8,4,8,512]{3,2,1,0:T(8,128)} %get-tuple-element.17, f32[8,4,8,512]{3,2,1,0:T(8,128)S(1)} %convolution_subtract_fusion.1, f32[512]{0:T(512)S(1)} %bitcast.91, ...), kind=kLoop, calls=%fused_computation.42 | loop fusion | flops 1572864 | bytes 2626560 | tf_op jit(solution)/shard_map/stack | solution.py:47
  81.7 0.8 %pad_maximum_fusion.1 = bf16[2,8,4,8,512]{4,3,2,1,0:T(8,128)(2,1)} fusion(bf16[1,8,4,8,512]{4,3,2,1,0:T(8,128)(2,1)S(1)} %get-tuple-element.8, bf16[1,8,4,8,512]{4,3,2,1,0:T(8,128)(2,1)S(1)} %get-tuple-element.7), kind=kLoop, calls=%fused_computation.8 | loop fusion | flops 262144 | bytes 1048576 | tf_op jit(solution)/shard_map/stack | solution.py:47
  (17 shorter events, 0.2 us)
Async XLA Ops:
  0.6 9.3 %copy-start = (bf16[2,512,512]{2,1,0:T(8,128)(2,1)S(1)}, bf16[2,512,512]{2,1,0:T(8,128)(2,1)}, u32[]{:S(2)}) copy-start(bf16[2,512,512]{2,1,0:T(8,128)(2,1)} %param.13) | copy-start | bytes 3145732
  3.0 5.5 %copy-start.7 = (s32[32]{0:T(128)S(1)}, s32[32]{0:T(128)}, u32[]{:S(2)}) copy-start(s32[32]{0:T(128)} %param.11) | copy-start | bytes 388
  3.0 6.9 %copy-start.1 = (bf16[2,8,4,8,512]{4,3,2,1,0:T(8,128)(2,1)S(1)}, bf16[2,8,4,8,512]{4,3,2,1,0:T(8,128)(2,1)}, u32[]{:S(2)}) copy-start(bf16[2,8,4,8,512]{4,3,2,1,0:T(8,128)(2,1)} %param.8) | copy-start | bytes 1572868
  3.0 17.6 %all-to-all-start = ((bf16[2,4,64,512]{3,1,0,2:T(4,128)(2,1)}), bf16[2,4,64,512]{3,1,0,2:T(4,128)(2,1)S(1)}, u32[]{:S(2)}, u32[]{:S(2)}) async-start(bf16[2,4,64,512]{3,1,0,2:T(4,128)(2,1)} %bitcast.84), calls=%async_computation | async-start | bytes 1048576 | tf_op jit(solution)/shard_map/all_to_all | solution.py:22
  8.4 0.7 copy-start.8
  9.2 0.7 copy-start.3
  22.4 4.4 %copy-start.5 = (s32[8,4,8]{2,1,0:T(4,128)S(1)}, s32[8,4,8]{2,1,0:T(4,128)}, u32[]{:S(2)}) copy-start(s32[8,4,8]{2,1,0:T(4,128)} %param.10) | copy-start | bytes 3076
  22.4 11.8 %all-to-all-start.1 = ((bf16[4,2,1,8,8,512]{5,4,3,1,2,0:T(8,128)(2,1)}), bf16[4,2,1,8,8,512]{5,4,3,1,2,0:T(8,128)(2,1)S(1)}, u32[]{:S(2)}, u32[]{:S(2)}) async-start(bf16[4,2,1,8,8,512]{5,4,3,1,2,0:T(8,128)(2,1)} %pad_maximum_fusion), calls=%async_computation.1 | async-start | bytes 1048576 | tf_op jit(solution)/shard_map/all_to_all | solution.py:26
  35.8 1.0 %copy-start.2 = (f32[8,4,8,512]{3,2,1,0:T(8,128)S(1)}, f32[8,4,8,512]{3,2,1,0:T(8,128)}, u32[]{:S(2)}) copy-start(f32[8,4,8,512]{3,2,1,0:T(8,128)} %fusion.2) | copy-start | bytes 1572868
  36.9 43.0 %copy-start.6 = (f32[512]{0:T(512)S(1)}, f32[512]{0:T(512)}, u32[]{:S(2)}) copy-start(f32[512]{0:T(512)} %param.15) | copy-start | bytes 6148
  79.9 0.6 copy-start.4
